TPU v7x, 128 devices: a whole 4x4x4 slice. The times are simulated.
128 devices in a mesh: req: 16 (over y, z), mdl: 8 (over x, core).
Axes of the slice: x: 4, y: 4, z: 4, core: 2. Of those that a mesh axis runs over, the one named last changes fastest.
Arguments:
- segments: int32 [1024], P('req'), may hold values from -1 to 1023, as said below
- queries: bfloat16 [1024, 8192], P('req', 'mdl'), may hold values from -200 to 200
- keys_values: bfloat16 [1024, 2, 1024], P('req', None, 'mdl'), may hold values from -6 to 6
- page_table: int32 [64], replicated, may hold values from 0 to 127, as said below
- paged_cache: bfloat16 [128, 16, 2, 1024], P('req', None, None, 'mdl'), may hold values from -6 to 6
- residual: bfloat16 [1024, 8192], P(None, 'req'), may hold values from -40 to 40
- out_weight: bfloat16 [8192, 8192], P('mdl', 'req'), may hold values from -0.0625 to 0.0625
- norm_gain: bfloat16 [8192], P('req'), may hold values from 0.099609375 to 1.8984375
- gate_up_weight: bfloat16 [8192, 2, 29568], P('req', None, 'mdl'), may hold values from -0.0625 to 0.0625
Outputs:
- hidden: bfloat16 [1024, 29568], P('req', 'mdl')
- cache_new: bfloat16 [128, 16, 2, 1024], P('req', None, None, 'mdl')
Inputs may be any that keep to these rules, and one draw needn't show every extreme that they name: `segments`: each block of 64 slots of one index of req holds whole requests followed by pads; a live slot's entry is the slot index of its request's first slot, in that block; in every draw some block has no pads. `page_table`: all entries differ; page p lies on index p // 8 of req; the pages of one block of 64 slots all lie on one index of req, and different blocks on different indices.
All inputs are finite; a program needn't handle non-finite values.
Results may differ from a plain program's by a relative error of at most 0.024.
Values may be sent and summed in bfloat16 or wider, within the bound.
A program may use at most 128 MiB of HBM per device.

v0:
```python
import jax
import jax.numpy as jnp
from jax import lax
from jax.sharding import PartitionSpec as P

D = 8192
HD = 128
QPK = 8
PAGE = 16
EPSILON = 1e-06


def attention_block(query_rows, pair_rows, seg_rows):
    slots = seg_rows.shape[0]
    groups = pair_rows.shape[2] // HD
    query = query_rows.reshape(slots, groups, QPK, HD)
    keys = pair_rows[:, 0].reshape(slots, groups, HD)
    values = pair_rows[:, 1].reshape(slots, groups, HD)
    scores = jnp.einsum("igqd,jgd->gqij", query, keys, preferred_element_type=jnp.float32) * HD ** (
        -0.5
    )
    places = jnp.arange(slots, dtype=jnp.int32)
    allowed = (
        (seg_rows[:, None] == seg_rows[None, :])
        & (seg_rows[:, None] >= 0)
        & (places[None, :] < places[:, None])
    )
    allowed = allowed | (places[:, None] == places[None, :])
    scores = jnp.where(allowed, scores, -jnp.inf)
    highest = jnp.max(scores, axis=-1, keepdims=True)
    weights = jnp.exp(scores - highest)
    probs = (weights / jnp.sum(weights, axis=-1, keepdims=True)).astype(jnp.bfloat16)
    mixed = jnp.einsum("gqij,jgd->igqd", probs, values, preferred_element_type=jnp.float32)
    mixed = jnp.where((seg_rows >= 0)[:, None, None, None], mixed, 0.0)
    return mixed.reshape(slots, groups * QPK * HD).astype(jnp.bfloat16)


def on_device(
    segments,
    queries,
    keys_values,
    page_table,
    paged_cache,
    residual,
    out_weight,
    norm_gain,
    gate_up_weight,
):
    attended = attention_block(queries, keys_values, segments)
    live_rows = (segments >= 0).astype(jnp.bfloat16)
    every_pair, every_live = (
        lax.all_gather(keys_values, "req", axis=0, tiled=True),
        lax.all_gather(live_rows, "req", axis=0, tiled=True),
    )
    local_pages = paged_cache.shape[0]
    slot_count = every_pair.shape[0]
    token_pages = jnp.repeat(page_table, PAGE, total_repeat_length=slot_count)
    target = token_pages - lax.axis_index("req") * local_pages
    writable = (target >= 0) & (target < local_pages) & (every_live > 0)
    target = jnp.where(writable, target, local_pages)
    offsets = jnp.arange(slot_count, dtype=jnp.int32) % PAGE
    cache_new = paged_cache.at[target, offsets].set(every_pair, mode="drop")
    partial_value = jnp.dot(
        lax.all_gather(attended, "req", axis=0, tiled=True),
        out_weight,
        preferred_element_type=jnp.float32,
    )
    gain_row = norm_gain.astype(jnp.float32)
    stream = residual.astype(jnp.float32) + lax.psum(
        partial_value.astype(jnp.bfloat16), "mdl"
    ).astype(jnp.float32)
    squares = jnp.sum(stream * stream, axis=1)
    totals = lax.psum(squares, "req")
    normed = (stream * lax.rsqrt(totals / D + EPSILON)[:, None] * gain_row[None, :]).astype(
        jnp.bfloat16
    )
    flat_weight = gate_up_weight.reshape(gate_up_weight.shape[0], -1)
    summed = lax.psum_scatter(
        jnp.dot(normed, flat_weight, preferred_element_type=jnp.float32).astype(jnp.bfloat16),
        "req",
        scatter_dimension=0,
        tiled=True,
    ).astype(jnp.float32)
    split_at = summed.shape[1] // 2
    hidden = (jax.nn.silu(summed[:, :split_at]) * summed[:, split_at:]).astype(jnp.bfloat16)
    return (hidden, cache_new)


def solution(mesh):
    placed = (
        P("req"),
        P("req", "mdl"),
        P("req", None, "mdl"),
        P(),
        P("req", None, None, "mdl"),
        P(None, "req"),
        P("mdl", "req"),
        P("req"),
        P("req", None, "mdl"),
    )
    return jax.shard_map(
        on_device,
        mesh=mesh,
        in_specs=placed,
        out_specs=(P("req", "mdl"), P("req", None, None, "mdl")),
        check_vma=False,
    )
```

profile of v0, /device:TPU:0, one launch (start us, length us, event | category | flops | bytes accessed | tf_op | source)
XLA Modules:
  0.0 327.5 jit_solution(5003735953313754061)
XLA Ops:
  7.2 0.0 copy-start
  7.2 0.0 all-gather.2.cloned.1.call-start
  7.2 0.9 fusion.16
  8.1 0.7 fusion.15
  8.8 0.8 fusion.13
  9.6 1.2 fusion.21
  10.8 0.1 fusion.8
  10.9 0.2 fusion.4
  11.1 0.1 copy.24
  11.2 0.7 copy.43
  11.9 0.0 all-gather.2.cloned.1.call-update
  11.9 0.0 copy-start.8
  11.9 0.0 copy-start.4
  11.9 0.0 all-reduce.3.cloned.1.call-start
  12.0 47.6 %all-gather.2.cloned.1.call-done = bf16[1024,1024]{1,0:T(8,128)(2,1)} async-done(((bf16[64,1024]{1,0:T(8,128)(2,1)}), bf16[1024,1024]{1,0:T(8,128)(2,1)}) %all-gather.2.cloned.1.call-update) | async-done | bytes 2097168 | tf_op jit(solution)/shard_map/all_gather | solution.py:64
  59.6 0.0 copy-done
  59.6 3.8 %convolution_convert_fusion.1 = bf16[1024,512]{1,0:T(8,128)(2,1)} fusion(bf16[1024,1024]{1,0:T(8,128)(2,1)} %all-gather.2.cloned.1.call-done, bf16[1024,512]{1,0:T(8,128)(2,1)S(1)} %copy-done), kind=kOutput, calls=%fused_computation.5 | convolution fusion | flops 1074266112 | bytes 4194304 | tf_op jit(solution)/shard_map/dot_general | solution.py:63
  63.4 0.0 all-reduce.3.cloned.1.call-update
  63.4 0.0 reduce-scatter.2.cloned.1.call-start
  63.5 0.0 copy-done.8
  63.5 61.8 %all-reduce.3.cloned.1.call-done = bf16[1024,512]{1,0:T(8,128)(2,1)} async-done(((bf16[1024,512]{1,0:T(8,128)(2,1)}), bf16[1024,512]{1,0:T(8,128)(2,1)}) %all-reduce.3.cloned.1.call-update) | async-done | bytes 1048592 | tf_op jit(solution)/shard_map/psum | solution.py:69
  125.3 1.7 multiply_reduce_fusion
  127.1 40.6 %psum.15 = f32[1024]{0:T(1024)S(1)} all-reduce(f32[1024]{0:T(1024)S(1)} %multiply_reduce_fusion), channel_id=1, replica_groups=mesh['req'=16,'mdl'=8] {'req'}, use_global_device_ids=true, to_apply=%region_4.5 | all-reduce | flops 1024 | bytes 8192 | tf_op jit(solution)/shard_map/psum | solution.py:73
  167.7 14.8 %convolution_convert_fusion = bf16[1024,7392]{1,0:T(8,128)(2,1)} fusion(bf16[512,7392]{0,1:T(8,128)(2,1)} %bitcast.142, bf16[1024,512]{1,0:T(8,128)(2,1)S(1)} %copy-done.5, bf16[1024,512]{1,0:T(8,128)(2,1)S(1)} %copy-done.4, f32[512]{0:T(512)S(1)} %convert_element_type.46, f32[1024]{0:T(1024)S(1)} %add_rsqrt_fusion), kind=kOutput, calls=%fused_computation.1 | convolution fusion | flops 7761788928 | bytes 24811520 | tf_op jit(solution)/shard_map/dot_general | solution.py:79
  182.4 0.0 copy-start.9
  182.4 0.0 copy-start.6
  182.4 0.0 copy-start.2
  182.5 0.0 reduce-scatter.2.cloned.1.call-update
  182.5 0.6 copy-done.11
  183.1 0.6 dynamic-slice.6
  184.3 0.2 dynamic-update-slice.3
  184.5 36.8 %all-reduce = bf16[1024]{0:T(1024)(128)(2,1)S(1)} all-reduce(bf16[1024]{0:T(1024)(128)(2,1)S(1)} %dynamic-update-slice.3), channel_id=1, replica_groups=mesh['req'=16,'mdl'=8] {'req'}, use_global_device_ids=true, to_apply=%add | all-reduce | flops 1024 | bytes 4096
  221.3 0.7 fusion.20
  222.0 0.7 fusion.19
  222.7 0.7 fusion.17
  223.4 0.7 fusion.18
  224.2 0.1 add_add_fusion.1
  224.3 4.4 %compare_select_fusion.2 = (s32[1024,1]{0,1:T(1,128)S(1)}, s32[1024,1]{0,1:T(1,128)S(1)}) fusion(s32[]{:T(128)} %bitcast.73, s32[]{:T(128)} %bitcast.74, s32[]{:T(128)} %bitcast.75, s32[]{:T(128)} %bitcast.76, s32[]{:T(128)} %bitcast.77, s32[]{:T(128)} %bitcast.79, s32[]{:T(128)} %bitcast.78, s32[1024,1]{0,1:T(1,128)S(1)} %bitcast.141, ...), kind=kLoop, calls=%fused_computation.89 | loop fusion | flops 14336 | bytes 16412 | tf_op jit(solution)/shard_map/jit(_take)/gather | solution.py:57
  228.6 0.7 compare_reduce_fusion.56
  229.4 35.7 %compare_select_fusion.8 = s32[1024]{0:T(1024)S(1)} fusion(bf16[1024]{0:T(1024)(128)(2,1)S(1)} %all-reduce, pred[1024]{0:T(1024)(128)(4,1)S(1)} %get-tuple-element.70, pred[1024]{0:T(1024)(128)(4,1)S(1)} %get-tuple-element.69, pred[1024]{0:T(1024)(128)(4,1)S(1)} %get-tuple-element.68, pred[1024]{0:T(1024)(128)(4,1)S(1)} %get-tuple-element.67, ...), kind=kLoop, calls=%fused_computation.97 | loop fusion | flops 79872 | bytes 72968 | tf_op jit(solution)/shard_map/select_n | solution.py:62
  265.1 0.1 multiply_reduce_fusion.1
  265.2 0.1 and_reduce_fusion
  265.3 23.3 %all_gather.11 = bf16[1024,2,128]{2,1,0:T(2,128)(2,1)S(1)} all-gather(bf16[64,2,128]{2,1,0:T(2,128)(2,1)S(1)} %copy-done.6), channel_id=1, replica_groups=mesh['req'=16,'mdl'=8] {'req'}, dimensions={0}, use_global_device_ids=true | all-gather | bytes 557056 | tf_op jit(solution)/shard_map/all_gather | solution.py:52
  288.6 29.9 %scatter_fusion = bf16[128,2,128]{2,1,0:T(2,128)(2,1)S(1)} fusion(bf16[128,2,128]{2,1,0:T(2,128)(2,1)S(1)} %bitcast.134, s32[1024]{0:T(1024)S(1)} %broadcast_select_fusion, bf16[1024,2,128]{2,1,0:T(2,128)(2,1)S(1)} %all_gather.11), kind=kCustom, calls=%fused_computation | custom fusion | bytes 1576960
  318.5 0.0 copy-start.1
  318.6 0.0 reduce-scatter.2.cloned.1.call-done
  318.6 1.3 convert_element_type.49
  319.9 1.1 fusion.7
  (20 shorter events, 0.1 us)
Async XLA Ops:
  7.2 52.4 %copy-start = (bf16[1024,512]{1,0:T(8,128)(2,1)S(1)}, bf16[1024,512]{1,0:T(8,128)(2,1)}, u32[]{:S(2)}) copy-start(bf16[1024,512]{1,0:T(8,128)(2,1)} %param.17) | copy-start | bytes 3145732
  7.2 52.4 %all-gather.2.cloned.1.call-start = ((), (), s32[]{:S(2)}) async-start(), calls=%async_computation.1 | async-start | bytes 2228224 | tf_op jit(solution)/shard_map/all_gather | solution.py:64
  11.9 51.6 %copy-start.8 = (bf16[512]{0:T(512)(128)(2,1)S(1)}, bf16[512]{0:T(512)(128)(2,1)}, u32[]{:S(2)}) copy-start(bf16[512]{0:T(512)(128)(2,1)} %param.18) | copy-start | bytes 3076
  11.9 113.4 %copy-start.4 = (bf16[1024,512]{1,0:T(8,128)(2,1)S(1)}, bf16[1024,512]{1,0:T(8,128)(2,1)}, u32[]{:S(2)}) copy-start(bf16[1024,512]{1,0:T(8,128)(2,1)} %param.16) | copy-start | bytes 3145732
  11.9 113.4 %all-reduce.3.cloned.1.call-start = ((), (), s32[]{:S(2)}) async-start(), calls=%async_computation.2 | async-start | bytes 2097152 | tf_op jit(solution)/shard_map/psum | solution.py:69
  63.4 255.1 %reduce-scatter.2.cloned.1.call-start = ((), (), s32[]{:S(2)}) async-start(), calls=%async_computation.3 | async-start | bytes 16154624 | tf_op jit(solution)/shard_map/reduce_scatter | solution.py:78
  125.3 42.3 %copy-start.5 = (bf16[1024,512]{1,0:T(8,128)(2,1)S(1)}, bf16[1024,512]{1,0:T(8,128)(2,1)}, u32[]{:S(2)}) copy-start(bf16[1024,512]{1,0:T(8,128)(2,1)} %all-reduce.3.cloned.1.call-done) | copy-start | bytes 3145732
  182.4 0.7 copy-start.11
  182.4 38.9 %copy-start.3 = (s32[64]{0:T(128)S(1)}, s32[64]{0:T(128)}, u32[]{:S(2)}) copy-start(s32[64]{0:T(128)} %param.14) | copy-start | bytes 772
  182.4 41.8 %copy-start.7 = (s32[8,128]{1,0:T(8,128)S(1)}, s32[8,128]{1,0:T(8,128)}, u32[]{:S(2)}) copy-start(s32[8,128]{1,0:T(8,128)} %constant.119.clone.1) | copy-start | bytes 12292
  182.4 82.7 %copy-start.10 = (s32[2]{0:T(128)S(1)}, s32[2]{0:T(128)}, u32[]{:S(2)}) copy-start(s32[2]{0:T(128)} %constant.129) | copy-start | bytes 28
  182.4 82.8 %copy-start.9 = (s32[2]{0:T(128)S(1)}, s32[2]{0:T(128)}, u32[]{:S(2)}) copy-start(s32[2]{0:T(128)} %constant.132) | copy-start | bytes 28
  182.4 82.9 %copy-start.6 = (bf16[64,2,128]{2,1,0:T(2,128)(2,1)S(1)}, bf16[64,2,128]{2,1,0:T(2,128)(2,1)}, u32[]{:S(2)}) copy-start(bf16[64,2,128]{2,1,0:T(2,128)(2,1)} %param.13) | copy-start | bytes 98308
  182.4 106.1 %copy-start.2 = (bf16[8,16,2,128]{3,2,1,0:T(2,128)(2,1)S(1)}, bf16[8,16,2,128]{3,2,1,0:T(2,128)(2,1)}, u32[]{:S(2)}) copy-start(bf16[8,16,2,128]{3,2,1,0:T(2,128)(2,1)} %param.15) | copy-start | bytes 196612
  318.5 2.5 copy-start.1
Sparse Core Ops, SparseCore 0:
  12.0 47.5 all-gather.1
  63.6 61.7 all-reduce.2
  182.6 99.0 reduce-scatter.1
where the time goes:
time: 328 us
  waiting for transfers between devices  110 us (34%)
  blocking collectives  101 us (31%)
  other arithmetic  46.8 us (14%)
  local copies, waits for them, and re-layouts  35.9 us (11%)
  matrix products  20 us (6%)
  between operations  14.6 us (4%)
    psum x1, waiting for transfers between devices, on_device(): lax.psum(partial_value.astype(jnp.bfloat16), 'mdl').astype(jnp.float32)  61.8 us
    all_gather x1, waiting for transfers between devices, on_device(): lax.all_gather(attended, 'req', axis=0, tiled=True)  47.6 us
    psum x1, blocking collectives, on_device(): totals = lax.psum(squares, 'req')  40.6 us
    unnamed x1, blocking collectives  36.8 us
    select_n x2, other arithmetic, on_device(): cache_new = paged_cache.at[target, offsets].set(every_pair, mode='drop')  35.7 us
    unnamed x29, local copies, waits for them, and re-layouts  32.1 us
    all_gather x1, blocking collectives, on_device(): lax.all_gather(keys_values, 'req', axis=0, tiled=True)  23.3 us
    dot_general x1, matrix products, on_device(): jnp.dot(normed, flat_weight, preferred_element_type=jnp.float32)  14.8 us
  transfers between devices with their start and end apart: 3, of which 2 were waited for; matrix products, arithmetic and copies ran while one was open for 23% of the time, Pallas kernels for 0%

commit v1 on v0

--- a/solution.py
+++ b/solution.py
@@ -8,6 +8,11 @@
 QPK = 8
 PAGE = 16
 EPSILON = 1e-06
+
+
+def gather_from_all(x, axis, dim):
+    copies = jnp.concatenate([x] * lax.axis_size(axis), axis=dim)
+    return lax.all_to_all(copies, axis, dim, dim, tiled=True)
 
 
 def attention_block(query_rows, pair_rows, seg_rows):
@@ -61,9 +66,7 @@
     offsets = jnp.arange(slot_count, dtype=jnp.int32) % PAGE
     cache_new = paged_cache.at[target, offsets].set(every_pair, mode="drop")
     partial_value = jnp.dot(
-        lax.all_gather(attended, "req", axis=0, tiled=True),
-        out_weight,
-        preferred_element_type=jnp.float32,
+        gather_from_all(attended, "req", 0), out_weight, preferred_element_type=jnp.float32
     )
     gain_row = norm_gain.astype(jnp.float32)
     stream = residual.astype(jnp.float32) + lax.psum(

time: 328 us -> 315 us (0.960)
  waiting for transfers between devices: 110 us -> 60.8 us
  blocking collectives: 101 us -> 137 us
    all_gather x1 -> x0, waiting for transfers between devices: 47.6 us -> none  [on_device(): lax.all_gather(attended, 'req', axis=0, tiled=True)]
    all_to_all x0 -> x1, blocking collectives: none -> 36.2 us  [gather_from_all(): return lax.all_to_all(copies, axis, dim, dim, tiled=True)]
    unnamed x29 -> x43, local copies, waits for them, and re-layouts: 32.1 us -> 31.7 us
  transfers between devices with their start and end apart: 3 -> 2, of which waited for: 2 -> 1; matrix products, arithmetic and copies ran while one was open for 23% -> 24% of each run, Pallas kernels for 0% -> 0%
where the time goes in v1:
time: 315 us; the launch traced here: 314 us
  blocking collectives  137 us (43%)
  waiting for transfers between devices  60.8 us (19%)
  other arithmetic  46.8 us (15%)
  local copies, waits for them, and re-layouts  35.5 us (11%)
  matrix products  18.4 us (6%)
  between operations  15 us (5%)
    psum x1, waiting for transfers between devices, on_device(): lax.psum(partial_value.astype(jnp.bfloat16), 'mdl').astype(jnp.float32)  60.8 us
    psum x1, blocking collectives, on_device(): totals = lax.psum(squares, 'req')  40.6 us
    unnamed x1, blocking collectives  36.7 us
    all_to_all x1, blocking collectives, gather_from_all(): return lax.all_to_all(copies, axis, dim, dim, tiled=True)  36.2 us
    select_n x2, other arithmetic, on_device(): cache_new = paged_cache.at[target, offsets].set(every_pair, mode='drop')  35.7 us
    unnamed x43, local copies, waits for them, and re-layouts  31.7 us
    all_gather x1, blocking collectives, on_device(): lax.all_gather(keys_values, 'req', axis=0, tiled=True)  23.4 us
    dot_general x1, matrix products, on_device(): jnp.dot(normed, flat_weight, preferred_element_type=jnp.float32)  14.8 us
  transfers between devices with their start and end apart: 2, of which 1 were waited for; matrix products, arithmetic and copies ran while one was open for 24% of the time, Pallas kernels for 0%

profile of v1, /device:TPU:0, one launch (start us, length us, event | category | flops | bytes accessed | tf_op | source)
XLA Modules:
  0.0 313.6 jit_solution(17197051607608939252)
XLA Ops:
  7.2 0.0 copy-start
  7.2 0.0 all-reduce.3.cloned.1.call-start
  7.2 0.7 fusion.15
  8.0 0.8 fusion.13
  8.8 0.9 fusion.16
  9.7 1.2 fusion.21
  10.8 0.1 fusion.8
  10.9 0.2 fusion.4
  11.2 0.1 copy.24
  11.7 36.2 %all_to_all.12 = bf16[16,64,1024]{2,1,0:T(8,128)(2,1)S(1)} all-to-all(bf16[16,64,1024]{2,1,0:T(8,128)(2,1)S(1)} %bitcast.167), channel_id=1, replica_groups=mesh['req'=16,'mdl'=8] {'req'}, dimensions={0} | all-to-all | bytes 4194304 | tf_op jit(solution)/shard_map/all_to_all | solution.py:15
  47.9 0.0 copy-done
  47.9 2.3 convolution_convert_fusion.1
  50.2 0.0 all-reduce.3.cloned.1.call-update
  50.2 0.0 reduce-scatter.2.cloned.1.call-start
  50.2 0.0 copy-done.8
  50.3 60.8 %all-reduce.3.cloned.1.call-done = bf16[1024,512]{1,0:T(8,128)(2,1)} async-done(((bf16[1024,512]{1,0:T(8,128)(2,1)}), bf16[1024,512]{1,0:T(8,128)(2,1)}) %all-reduce.3.cloned.1.call-update) | async-done | bytes 1048592 | tf_op jit(solution)/shard_map/psum | solution.py:72
  111.0 0.0 copy-done.4
  111.0 1.7 multiply_reduce_fusion
  112.8 40.6 %psum.15 = f32[1024]{0:T(1024)S(1)} all-reduce(f32[1024]{0:T(1024)S(1)} %multiply_reduce_fusion), channel_id=1, replica_groups=mesh['req'=16,'mdl'=8] {'req'}, use_global_device_ids=true, to_apply=%region_4.5 | all-reduce | flops 1024 | bytes 8192 | tf_op jit(solution)/shard_map/psum | solution.py:76
  153.4 0.0 copy-done.5
  153.4 14.8 %convolution_convert_fusion = bf16[1024,7392]{1,0:T(8,128)(2,1)} fusion(bf16[512,7392]{0,1:T(8,128)(2,1)} %bitcast.174, bf16[1024,512]{1,0:T(8,128)(2,1)S(1)} %copy-done.5, bf16[1024,512]{1,0:T(8,128)(2,1)S(1)} %copy-done.4, f32[512]{0:T(512)S(1)} %convert_element_type.46, f32[1024]{0:T(1024)S(1)} %add_rsqrt_fusion), kind=kOutput, calls=%fused_computation.1 | convolution fusion | flops 7761788928 | bytes 24811520 | tf_op jit(solution)/shard_map/dot_general | solution.py:82
  168.1 0.0 copy-start.9
  168.1 0.0 copy-start.6
  168.2 0.0 copy-start.2
  168.2 0.0 reduce-scatter.2.cloned.1.call-update
  168.2 0.6 copy-done.11
  168.8 0.6 dynamic-slice.6
  170.0 0.2 dynamic-update-slice.3
  170.3 36.7 %all-reduce = bf16[1024]{0:T(1024)(128)(2,1)S(1)} all-reduce(bf16[1024]{0:T(1024)(128)(2,1)S(1)} %dynamic-update-slice.3), channel_id=1, replica_groups=mesh['req'=16,'mdl'=8] {'req'}, use_global_device_ids=true, to_apply=%add | all-reduce | flops 1024 | bytes 4096
  206.9 0.0 copy-done.3
  206.9 0.7 fusion.20
  207.6 0.7 fusion.19
  208.3 0.7 fusion.17
  209.1 0.7 fusion.18
  209.8 0.1 add_add_fusion.1
  209.9 4.4 %compare_select_fusion.2 = (s32[1024,1]{0,1:T(1,128)S(1)}, s32[1024,1]{0,1:T(1,128)S(1)}) fusion(s32[]{:T(128)} %bitcast.75, s32[]{:T(128)} %bitcast.76, s32[]{:T(128)} %bitcast.77, s32[]{:T(128)} %bitcast.78, s32[]{:T(128)} %bitcast.79, s32[]{:T(128)} %bitcast.81, s32[]{:T(128)} %bitcast.80, s32[1024,1]{0,1:T(1,128)S(1)} %bitcast.173, ...), kind=kLoop, calls=%fused_computation.104 | loop fusion | flops 14336 | bytes 16412 | tf_op jit(solution)/shard_map/jit(_take)/gather | solution.py:62
  214.3 0.7 compare_reduce_fusion.56
  215.0 35.7 %compare_select_fusion.8 = s32[1024]{0:T(1024)S(1)} fusion(bf16[1024]{0:T(1024)(128)(2,1)S(1)} %all-reduce, pred[1024]{0:T(1024)(128)(4,1)S(1)} %get-tuple-element.70, pred[1024]{0:T(1024)(128)(4,1)S(1)} %get-tuple-element.69, pred[1024]{0:T(1024)(128)(4,1)S(1)} %get-tuple-element.68, pred[1024]{0:T(1024)(128)(4,1)S(1)} %get-tuple-element.67, ...), kind=kLoop, calls=%fused_computation.112 | loop fusion | flops 79872 | bytes 72968 | tf_op jit(solution)/shard_map/select_n | solution.py:67
  250.7 0.0 copy-done.10
  250.7 0.1 multiply_reduce_fusion.1
  250.8 0.1 and_reduce_fusion
  250.9 0.0 copy-done.6
  250.9 23.4 %all_gather.7 = bf16[1024,2,128]{2,1,0:T(2,128)(2,1)S(1)} all-gather(bf16[64,2,128]{2,1,0:T(2,128)(2,1)S(1)} %copy-done.6), channel_id=1, replica_groups=mesh['req'=16,'mdl'=8] {'req'}, dimensions={0}, use_global_device_ids=true | all-gather | bytes 557056 | tf_op jit(solution)/shard_map/all_gather | solution.py:57
  274.4 29.9 %scatter_fusion = bf16[128,2,128]{2,1,0:T(2,128)(2,1)S(1)} fusion(bf16[128,2,128]{2,1,0:T(2,128)(2,1)S(1)} %bitcast.166, s32[1024]{0:T(1024)S(1)} %broadcast_select_fusion, bf16[1024,2,128]{2,1,0:T(2,128)(2,1)S(1)} %all_gather.7), kind=kCustom, calls=%fused_computation | custom fusion | bytes 1576960
  304.3 0.0 copy-start.1
  304.3 0.0 reduce-scatter.2.cloned.1.call-done
  304.4 1.3 convert_element_type.49
  305.7 1.1 fusion.7
  (33 shorter events, 0.3 us)
Async XLA Ops:
  7.2 40.7 %copy-start = (bf16[1024,512]{1,0:T(8,128)(2,1)S(1)}, bf16[1024,512]{1,0:T(8,128)(2,1)}, u32[]{:S(2)}) copy-start(bf16[1024,512]{1,0:T(8,128)(2,1)} %param.17) | copy-start | bytes 3145732
  7.2 103.9 %all-reduce.3.cloned.1.call-start = ((), (), s32[]{:S(2)}) async-start(), calls=%async_computation.2 | async-start | bytes 2097152 | tf_op jit(solution)/shard_map/psum | solution.py:72
  47.9 2.4 copy-start.8
  47.9 63.2 %copy-start.4 = (bf16[1024,512]{1,0:T(8,128)(2,1)S(1)}, bf16[1024,512]{1,0:T(8,128)(2,1)}, u32[]{:S(2)}) copy-start(bf16[1024,512]{1,0:T(8,128)(2,1)} %param.16) | copy-start | bytes 3145732
  50.2 254.2 %reduce-scatter.2.cloned.1.call-start = ((), (), s32[]{:S(2)}) async-start(), calls=%async_computation.3 | async-start | bytes 16154624 | tf_op jit(solution)/shard_map/reduce_scatter | solution.py:81
  111.0 42.3 %copy-start.5 = (bf16[1024,512]{1,0:T(8,128)(2,1)S(1)}, bf16[1024,512]{1,0:T(8,128)(2,1)}, u32[]{:S(2)}) copy-start(bf16[1024,512]{1,0:T(8,128)(2,1)} %all-reduce.3.cloned.1.call-done) | copy-start | bytes 3145732
  168.1 0.7 copy-start.11
  168.1 38.8 %copy-start.3 = (s32[64]{0:T(128)S(1)}, s32[64]{0:T(128)}, u32[]{:S(2)}) copy-start(s32[64]{0:T(128)} %param.14) | copy-start | bytes 772
  168.1 41.7 %copy-start.7 = (s32[8,128]{1,0:T(8,128)S(1)}, s32[8,128]{1,0:T(8,128)}, u32[]{:S(2)}) copy-start(s32[8,128]{1,0:T(8,128)} %constant.119.clone.1) | copy-start | bytes 12292
  168.1 82.6 %copy-start.10 = (s32[2]{0:T(128)S(1)}, s32[2]{0:T(128)}, u32[]{:S(2)}) copy-start(s32[2]{0:T(128)} %constant.129) | copy-start | bytes 28
  168.1 82.7 %copy-start.9 = (s32[2]{0:T(128)S(1)}, s32[2]{0:T(128)}, u32[]{:S(2)}) copy-start(s32[2]{0:T(128)} %constant.132) | copy-start | bytes 28
  168.1 82.8 %copy-start.6 = (bf16[64,2,128]{2,1,0:T(2,128)(2,1)S(1)}, bf16[64,2,128]{2,1,0:T(2,128)(2,1)}, u32[]{:S(2)}) copy-start(bf16[64,2,128]{2,1,0:T(2,128)(2,1)} %param.13) | copy-start | bytes 98308
  168.2 106.2 %copy-start.2 = (bf16[8,16,2,128]{3,2,1,0:T(2,128)(2,1)S(1)}, bf16[8,16,2,128]{3,2,1,0:T(2,128)(2,1)}, u32[]{:S(2)}) copy-start(bf16[8,16,2,128]{3,2,1,0:T(2,128)(2,1)} %param.15) | copy-start | bytes 196612
  304.3 2.5 copy-start.1
Sparse Core Ops, SparseCore 0:
  50.3 60.6 all-reduce.2
  168.3 98.8 reduce-scatter.1
